TPU v7x, 256 devices: a whole 4x4x8 slice. The times are simulated.
256 devices in a mesh: group: 8 (over z_lo, x), member: 32 (over z_hi, y, core).
Axes of the slice: x: 4, y: 4, z: 8 (z_hi: 4, z_lo: 2; z = z_hi * 2 + z_lo), core: 2. Of those that a mesh axis runs over, the one named last changes fastest.
Arguments:
- entities: bfloat16 [131072, 400], P(('group', 'member')), may hold values from -1.796875 to 1.796875
- hub_rows: bfloat16 [128, 400], replicated, may hold values from -1.796875 to 1.796875
- relations: float32 [2112, 400], replicated
- matching: int32 [8], replicated, may hold values from 0 to 7, as said below
- head_index: int32 [4096, 256], P(('group', 'member')), may hold values from 0 to 511
- tail_index: int32 [4096, 256], P(('group', 'member')), may hold values from 0 to 639
- tile_rel: int32 [4096], P(('group', 'member')), may hold values from 0 to 2111
- tile_count: int32 [8, 32], P('group', 'member'), may hold values from 1 to 16, as said below
Outputs:
- new_entities: bfloat16 [131072, 400], P(('group', 'member'))
- new_hub: bfloat16 [128, 400], replicated
Inputs may be any that keep to these rules, and one draw needn't show every extreme that they name: `matching`: a permutation of the partitions. `tile_count`: some device has exactly 16 live tiles.
All inputs are finite; a program needn't handle non-finite values.
Results may differ from a plain program's by a relative error of at most 0.014.
Values may be sent and summed in bfloat16 or wider, within the bound.
No kernel may reach another device: no remote copies, remote signals or barrier semaphores. Data moves between devices by JAX's collectives and lax.ppermute only.
A program may use at most 64 MiB of HBM per device.

v0:
```python
import jax
import jax.numpy as jnp
from jax import lax
from jax.sharding import PartitionSpec as P

learn_rate = 0.1
contract_first = (((0,), (0,)), ((), ()))
contract_last = (((1,), (1,)), ((), ()))


def rotate(rows, weight):
    half = rows.shape[1] // 2
    real_part = rows[:, :half]
    imag_part = rows[:, half:]
    w_real = weight[:half]
    w_imag = weight[half:]
    return jnp.concatenate(
        [real_part * w_real - imag_part * w_imag, real_part * w_imag + imag_part * w_real], axis=1
    )


def pullback(grads, weight):
    half = grads.shape[1] // 2
    d_real = grads[:, :half]
    d_imag = grads[:, half:]
    w_real = weight[:half]
    w_imag = weight[half:]
    return jnp.concatenate(
        [d_real * w_real + d_imag * w_imag, d_imag * w_real - d_real * w_imag], axis=1
    )


def tile_grads(head_pick, tail_pick, weight):
    query = rotate(head_pick.astype(jnp.float32), weight).astype(jnp.bfloat16)
    scores = lax.dot_general(query, tail_pick, contract_last, preferred_element_type=jnp.float32)
    top_score = jnp.max(scores, axis=1, keepdims=True)
    expo = jnp.exp(scores - top_score)
    probs = expo / jnp.sum(expo, axis=1, keepdims=True)
    diff = (probs - jnp.eye(scores.shape[0], dtype=jnp.float32)).astype(jnp.bfloat16)
    d_query = jnp.dot(diff, tail_pick, preferred_element_type=jnp.float32)
    d_tail = lax.dot_general(
        diff, query, contract_first, preferred_element_type=jnp.float32
    ).astype(jnp.bfloat16)
    d_head = pullback(d_query, weight).astype(jnp.bfloat16)
    return (d_head, d_tail)


def picker(wanted, group_ids, running, shard_rows):
    block_len = running.shape[0]
    positions = jnp.arange(shard_rows.shape[0], dtype=jnp.int32)
    source_group = positions // block_len
    keep_rows = jnp.any((source_group[:, None] == group_ids[None, :]) & wanted[None, :], axis=1)
    selected = jnp.where(keep_rows[:, None], shard_rows, jnp.zeros_like(shard_rows))
    return jax.ops.segment_sum(selected, positions % block_len, num_segments=block_len)


def shards(entities, hub_rows, relations, matching, head_index, tail_index, tile_rel, tile_count):
    row_total = entities.shape[0]
    my_group = lax.axis_index("group")
    group_ids = jnp.arange(matching.shape[0], dtype=jnp.int32)
    partner = jnp.sum(jnp.where(group_ids == my_group, matching, 0))
    partner_rows = picker(
        group_ids == partner,
        group_ids,
        jnp.zeros_like(entities),
        lax.all_gather(entities, "group", axis=0, tiled=True),
    )
    table = jnp.concatenate([partner_rows, hub_rows], axis=0)
    row_ids = jnp.arange(row_total, dtype=jnp.int32)
    table_ids = jnp.arange(table.shape[0], dtype=jnp.int32)
    tile_total = tile_count[0, 0]

    def one_tile(tile_pos, grads):
        head_ids = lax.dynamic_index_in_dim(head_index, tile_pos, 0, keepdims=False)
        tail_ids = lax.dynamic_index_in_dim(tail_index, tile_pos, 0, keepdims=False)
        rel_id = lax.dynamic_index_in_dim(tile_rel, tile_pos, 0, keepdims=False)
        weight = lax.dynamic_index_in_dim(relations, rel_id, 0, keepdims=False)
        head_hot = (head_ids[:, None] == row_ids[None, :]).astype(jnp.bfloat16)
        tail_hot = (tail_ids[:, None] == table_ids[None, :]).astype(jnp.bfloat16)
        head_pick = jnp.dot(head_hot, entities, preferred_element_type=jnp.float32).astype(
            jnp.bfloat16
        )
        tail_pick = jnp.dot(tail_hot, table, preferred_element_type=jnp.float32).astype(
            jnp.bfloat16
        )
        d_head, d_tail = tile_grads(head_pick, tail_pick, weight)
        head_acc = grads[0] + lax.dot_general(
            head_hot, d_head, contract_first, preferred_element_type=jnp.float32
        )
        tail_acc = grads[1] + lax.dot_general(
            tail_hot, d_tail, contract_first, preferred_element_type=jnp.float32
        )
        return (head_acc, tail_acc)

    start_grads = (jnp.zeros(entities.shape, jnp.float32), jnp.zeros(table.shape, jnp.float32))
    head_acc, tail_acc = lax.fori_loop(0, tile_total, one_tile, start_grads)
    back_rows = tail_acc[:row_total].astype(jnp.bfloat16)
    returned = picker(
        matching == my_group,
        group_ids,
        jnp.zeros_like(back_rows),
        lax.all_gather(back_rows, "group", axis=0, tiled=True),
    ).astype(jnp.float32)
    new_entities = (entities.astype(jnp.float32) - learn_rate * (head_acc + returned)).astype(
        jnp.bfloat16
    )
    hub_part = tail_acc[row_total:]
    hub_sum = lax.psum(hub_part, ("group", "member"))
    new_hub = (hub_rows.astype(jnp.float32) - learn_rate * hub_sum).astype(jnp.bfloat16)
    return (new_entities, new_hub)


def solution(mesh):
    placed = (
        P(("group", "member"), None),
        P(),
        P(),
        P(),
        P(("group", "member"), None),
        P(("group", "member"), None),
        P(("group", "member")),
        P("group", "member"),
    )
    return jax.shard_map(
        shards,
        mesh=mesh,
        in_specs=placed,
        out_specs=(P(("group", "member"), None), P()),
        check_vma=False,
    )
```

profile of v0, /device:TPU:64, one launch (start us, length us, event | category | flops | bytes accessed | tf_op | source)
XLA Modules:
  0.0 567.3 jit_solution(7446300842249257001)
XLA Ops:
  7.2 0.7 all-gather.3.cloned.1.call-update
  7.9 1.0 copy.20
  9.0 5.3 copy.21
  15.7 43.5 %all-gather.3.cloned.1.call-done = bf16[4096,400]{0,1:T(8,128)(2,1)} async-done(((bf16[512,400]{0,1:T(8,128)(2,1)}), bf16[4096,400]{0,1:T(8,128)(2,1)}) %all-gather.3.cloned.1.call-update) | async-done | bytes 3276816 | tf_op jit(solution)/shard_map/all_gather | solution.py:66
  59.2 2.1 broadcast_select_fusion.1
  61.4 5.0 copy.19
  66.4 25.8 %scatter_custom_fusion = bf16[512,400]{1,0:T(8,128)(2,1)S(1)} fusion(s32[4096]{0:T(1024)S(1)} %bitcast.37, bf16[4096,400]{1,0:T(8,128)(2,1)} %copy.19, bf16[]{:T(256)} %constant.67.clone.1), kind=kCustom, calls=%fused_computation.43 | custom fusion | flops 1638400 | bytes 410112 | tf_op jit(solution)/shard_map/scatter-add | solution.py:54
  92.2 0.9 pad_maximum_fusion.4
  93.3 9.5 %while.13 = (s32[]{:T(128)}, f32[512,400]{0,1:T(8,128)S(1)}, f32[640,400]{0,1:T(8,128)S(1)}, s32[]{:T(128)}, s32[16,256]{1,0:T(8,128)}, /*index=5*/bf16[512,400]...) while((s32[]{:T(128)}, f32[512,400]{0,1:T(8,128)S(1)}, ...), condition=%wide.region_6.7_spmd.clone, body=%wide.region_3.6_spmd.clone.sunk | while | flops 633636352 | bytes 8955389 | solution.py:96
  96.5 0.9 constant_dynamic-slice_fusion.6
  97.3 0.7 constant_dynamic-slice_fusion.5
  98.1 1.6 convolution_convert_fusion.4
  102.8 0.7 slice.30
  103.7 0.8 slice.51
  104.5 1.0 copy.18
  105.6 1.3 copy.23
  106.9 368.0 %all-reduce.2.cloned.1.call-done = f32[128,400]{0,1:T(8,128)} async-done(((f32[128,400]{0,1:T(8,128)}), f32[128,400]{0,1:T(8,128)}) %all-reduce.2.cloned.1.call-update) | async-done | bytes 204816 | tf_op jit(solution)/shard_map/psum | solution.py:108
  474.9 1.6 subtract_convert_fusion.7
  476.5 48.9 %all-gather.5.cloned.1.call-done = bf16[4096,400]{0,1:T(8,128)(2,1)} async-done(((bf16[512,400]{0,1:T(8,128)(2,1)}), bf16[4096,400]{0,1:T(8,128)(2,1)}) %all-gather.5.cloned.1.call-update) | async-done | bytes 3276816 | tf_op jit(solution)/shard_map/all_gather | solution.py:102
  525.4 2.1 broadcast_select_fusion
  527.5 5.0 copy.22
  532.5 25.8 %scatter_custom_fusion.1 = bf16[512,400]{1,0:T(8,128)(2,1)S(1)} fusion(s32[4096]{0:T(1024)S(1)} %bitcast.38, bf16[4096,400]{1,0:T(8,128)(2,1)} %copy.22, bf16[]{:T(256)} %constant.67.clone.1), kind=kCustom, calls=%fused_computation.41 | custom fusion | flops 1638400 | bytes 410112 | tf_op jit(solution)/shard_map/scatter-add | solution.py:54
  558.2 1.6 subtract_convert_fusion.6
  559.8 0.9 copy.24
  (29 shorter events, 5.0 us)
Async XLA Ops:
  7.2 52.1 %all-gather.3.cloned.1.call-start = ((), (), s32[]{:S(2)}) async-start(), calls=%async_computation | async-start | bytes 3686400 | tf_op jit(solution)/shard_map/all_gather | solution.py:66
  7.9 467.0 %all-reduce.2.cloned.1.call-start = ((), (), s32[]{:S(2)}) async-start(), calls=%async_computation.2 | async-start | bytes 409600 | tf_op jit(solution)/shard_map/psum | solution.py:108
  9.0 5.3 copy-start.2
  66.4 26.9 %copy-start = (bf16[512,400]{0,1:T(8,128)(2,1)S(1)}, bf16[512,400]{0,1:T(8,128)(2,1)}, u32[]{:S(2)}) copy-start(bf16[512,400]{0,1:T(8,128)(2,1)} %param.10) | copy-start | bytes 1228804
  66.4 26.9 %copy-start.3 = (s32[16]{0:T(128)S(1)}, s32[16]{0:T(128)}, u32[]{:S(2)}) copy-start(s32[16]{0:T(128)} %param.16) | copy-start | bytes 196
  102.8 372.1 %copy-start.1 = (bf16[128,400]{0,1:T(8,128)(2,1)S(1)}, bf16[128,400]{0,1:T(8,128)(2,1)}, u32[]{:S(2)}) copy-start(bf16[128,400]{0,1:T(8,128)(2,1)} %param.11) | copy-start | bytes 307204
  103.5 421.9 %all-gather.5.cloned.1.call-start = ((), (), s32[]{:S(2)}) async-start(), calls=%async_computation.1 | async-start | bytes 3686400 | tf_op jit(solution)/shard_map/all_gather | solution.py:102
Sparse Core Ops, SparseCore 0:
  9.8 49.3 all-gather.2
  103.6 371.2 all-reduce.1
  477.2 48.0 all-gather.4
where the time goes:
time: 573 us; the launch traced here: 567 us
  waiting for transfers between devices  461 us (80%)
  other arithmetic  61.7 us (11%)
  local copies, waits for them, and re-layouts  23.3 us (4%)
  between operations  13.9 us (2%)
    psum x1, waiting for transfers between devices, shards(): hub_sum = lax.psum(hub_part, ('group', 'member'))  368 us
    scatter-add x2, other arithmetic, picker(): jax.ops.segment_sum(selected, positions % block_len, num_segments=block_len)  51.6 us
    all_gather x1, waiting for transfers between devices, shards(): lax.all_gather(back_rows, 'group', axis=0, tiled=True)  48.9 us
    all_gather x1, waiting for transfers between devices, shards(): lax.all_gather(entities, 'group', axis=0, tiled=True)  43.5 us
  transfers between devices with their start and end apart: 3, of which 3 were waited for; matrix products, arithmetic and copies ran while one was open for 2% of the time, Pallas kernels for 0%

commit v1 on v0

v1 whole, which is shorter than its diff:
```python
import jax
import jax.numpy as jnp
from jax import lax
from jax.experimental import pallas as pl
from jax.experimental.pallas import tpu as pltpu
from jax.sharding import PartitionSpec as P

learn_rate = 0.1
BF = jnp.bfloat16
F32 = jnp.float32
LANES = 128
VMEM = pl.BlockSpec(memory_space=pltpu.VMEM)
SMEM = pl.BlockSpec(memory_space=pltpu.SMEM)


def hot(ids_ref, tile, rows):
    ids = ids_ref[pl.ds(tile, 1), :]
    row = lax.broadcasted_iota(jnp.int32, (rows, ids.shape[1]), 0)
    return jnp.where(row == ids, 1.0, 0.0).astype(BF)


def pick_lane(block, lane):
    lanes = lax.broadcasted_iota(jnp.int32, block.shape, 1)
    return jnp.sum(jnp.where(lanes == lane, block, 0.0), axis=1, keepdims=True)


def dot_nn(a, b):
    return lax.dot_general(a, b, (((1,), (0,)), ((), ())), preferred_element_type=F32)


def dot_nt(a, b):
    return lax.dot_general(a, b, (((1,), (1,)), ((), ())), preferred_element_type=F32)


def dot_tn(a, b):
    return lax.dot_general(a, b, (((0,), (0,)), ((), ())), preferred_element_type=F32)


def query_kernel(count, rel_ids, ent, rel, heads, query, weights, block):
    half = ent.shape[0] // 2
    rels = rel.shape[1]
    whole = rels // LANES
    rest = rels - whole * LANES
    weights[...] = jnp.zeros_like(weights)
    block[...] = jnp.zeros_like(block)

    @pl.loop(0, count[0, 0])
    def _(tile):
        rid = rel_ids[tile]
        at = rid // LANES

        @pl.when(at < whole)
        def _():
            block[...] = rel[:, pl.ds(pl.multiple_of(at * LANES, LANES), LANES)]

        if rest:

            @pl.when(at >= whole)
            def _():
                block[:, :rest] = rel[:, whole * LANES :]

        w = pick_lane(block[...], rid - at * LANES)
        lanes = lax.broadcasted_iota(jnp.int32, weights.shape, 1)
        weights[...] = jnp.where(lanes == tile, w, weights[...])
        head = dot_nn(ent[...], hot(heads, tile, ent.shape[1]))
        hr, hi = head[:half], head[half:]
        wr, wi = w[:half], w[half:]
        query[tile] = jnp.concatenate([hr * wr - hi * wi, hr * wi + hi * wr], axis=0).astype(BF)


def tail_kernel(count, query, partner, hub, tails, pick, diff, grads, table, acc):
    dim, rows = hub.shape[0], partner.shape[1]
    table[:, :rows] = partner[:dim]
    table[:, rows:] = hub[...]
    acc[...] = jnp.zeros_like(acc)

    @pl.loop(0, count[0, 0])
    def _(tile):
        tail_hot = hot(tails, tile, table.shape[1])
        tail = dot_nn(table[...], tail_hot).astype(BF)
        pick[tile] = tail
        q = query[tile]
        scores = dot_tn(tail, q)
        top = jnp.max(scores, axis=0, keepdims=True)
        expo = jnp.exp(scores - top)
        probs = expo * (1.0 / jnp.sum(expo, axis=0, keepdims=True))
        eye = lax.broadcasted_iota(jnp.int32, scores.shape, 0) == lax.broadcasted_iota(
            jnp.int32, scores.shape, 1
        )
        d = (probs - jnp.where(eye, 1.0, 0.0)).astype(BF)
        diff[tile] = d
        d_tail = dot_nt(q, d).astype(BF)
        acc[...] += dot_nt(d_tail, tail_hot)

    chunks, step = grads.shape[0], grads.shape[1]
    for c in range(chunks):
        n = min(step, dim - c * step)
        grads[c, :n] = acc[c * step : c * step + n].astype(BF)
        if n < step:
            grads[c, n:] = jnp.zeros((step - n, grads.shape[2]), BF)


def head_kernel(count, pick, diff, weights, heads, acc):
    half = acc.shape[0] // 2
    acc[...] = jnp.zeros_like(acc)

    @pl.loop(0, count[0, 0])
    def _(tile):
        d_query = dot_nn(pick[tile], diff[tile])
        w = pick_lane(weights[...], tile)
        dr, di = d_query[:half], d_query[half:]
        wr, wi = w[:half], w[half:]
        d_head = jnp.concatenate([dr * wr + di * wi, di * wr - dr * wi], axis=0).astype(BF)
        acc[...] += dot_nt(d_head, hot(heads, tile, acc.shape[1]))


def reorder_kernel(matching, rows, out):
    for g in range(out.shape[0]):
        out[g] = rows[matching[g]]


def return_kernel(matching, back, hub, out):
    rows = out.shape[2] - hub.shape[2]
    total = hub[0].astype(F32)
    for m in range(1, hub.shape[0]):
        total += hub[m].astype(F32)
    total = total.astype(BF)
    for g in range(out.shape[0]):
        out[matching[g], :, :rows] = back[g, :, :rows]
        out[g, :, rows:] = total


def call(kernel, out_shape, in_specs, flops, moved, scratch=(), exps=0):
    many = isinstance(out_shape, (list, tuple))
    return pl.pallas_call(
        kernel,
        out_shape=out_shape,
        in_specs=in_specs,
        out_specs=[VMEM] * len(out_shape) if many else VMEM,
        scratch_shapes=scratch,
        compiler_params=pltpu.CompilerParams(vmem_limit_bytes=32 * 1024 * 1024),
        cost_estimate=pl.CostEstimate(flops=flops, bytes_accessed=moved, transcendentals=exps),
    )


def make(groups, members):
    def shards(entities, hub_rows, relations, matching, head_index, tail_index, tile_rel, tile_count):
        ent, hub, rel = entities.T, hub_rows.T, relations.T
        dim, rows = ent.shape
        hubs = hub.shape[1]
        tiles, edges = head_index.shape
        step = -(-dim // (8 * groups)) * 8
        shape = jax.ShapeDtypeStruct

        cut = jnp.pad(ent, ((0, groups * step - dim), (0, 0))).reshape(groups, step, rows)
        cut = lax.all_to_all(cut, "group", 0, 0)
        cut = call(
            reorder_kernel, shape(cut.shape, BF), [SMEM, VMEM], 0, 4 * cut.size
        )(matching, cut)
        partner = lax.all_to_all(cut, "group", 0, 0).reshape(groups * step, rows)

        one = 2 * tiles * edges * dim
        query, weights = call(
            query_kernel,
            [shape((tiles, dim, edges), BF), shape((dim, LANES), F32)],
            [SMEM, SMEM, VMEM, VMEM, VMEM],
            one * rows,
            8 * rel.size,
            [pltpu.VMEM((dim, LANES), F32)],
        )(tile_count, tile_rel, ent, rel, head_index)
        pick, diff, grads = call(
            tail_kernel,
            [
                shape((tiles, dim, edges), BF),
                shape((tiles, edges, edges), BF),
                shape((groups, step, rows + hubs), BF),
            ],
            [SMEM, VMEM, VMEM, VMEM, VMEM],
            2 * one * (rows + hubs + edges),
            8 * tiles * dim * edges,
            [pltpu.VMEM((dim, rows + hubs), BF), pltpu.VMEM((dim, rows + hubs), F32)],
            tiles * edges * edges,
        )(tile_count, query, partner, hub, tail_index)
        head_acc = call(
            head_kernel,
            shape((dim, rows), F32),
            [SMEM, VMEM, VMEM, VMEM, VMEM],
            one * (rows + edges),
            6 * tiles * dim * edges,
        )(tile_count, pick, diff, weights, head_index)

        got = lax.all_to_all(grads, "group", 0, 0)
        part = jnp.sum(got[:, :, rows:].astype(F32), axis=0).astype(BF)
        parts = jnp.broadcast_to(part[None], (members,) + part.shape)
        parts = lax.all_to_all(parts, "member", 0, 0)
        sent = call(
            return_kernel, shape(got.shape, BF), [SMEM, VMEM, VMEM], 0, 4 * got.size
        )(matching, got, parts)
        last = lax.all_to_all(sent, "group", 0, 0).reshape(groups * step, rows + hubs)[:dim].astype(F32)
        new_entities = (ent.astype(F32) - learn_rate * (head_acc + last[:, :rows])).astype(BF)
        new_hub = (hub.astype(F32) - learn_rate * last[:, rows:]).astype(BF)
        return (new_entities.T, new_hub.T)

    return shards


def solution(mesh):
    placed = (
        P(("group", "member"), None),
        P(),
        P(),
        P(),
        P(("group", "member"), None),
        P(("group", "member"), None),
        P(("group", "member")),
        P("group", "member"),
    )
    return jax.shard_map(
        make(mesh.shape["group"], mesh.shape["member"]),
        mesh=mesh,
        in_specs=placed,
        out_specs=(P(("group", "member"), None), P()),
        check_vma=False,
    )
```

time: 573 us -> 115 us (0.20)
  waiting for transfers between devices: 461 us -> 9.8 us
  blocking collectives: 0 us -> 75.1 us
  other arithmetic: 61.7 us -> 2.71 us
  between operations: 13.9 us -> 1.47 us
  local copies, waits for them, and re-layouts: 23.3 us -> 11.9 us
  starting transfers between devices: 0.3 us -> 7.79 us
    psum x1 -> x0, waiting for transfers between devices: 368 us -> none  [shards(): hub_sum = lax.psum(hub_part, ('group', 'member'))]
    all_gather x2 -> x0, waiting for transfers between devices: 92.4 us -> none  [the longest x1 48.9 us: shards(): lax.all_gather(back_rows, 'group', axis=0, tiled=True)]
    all_to_all x0 -> x3, blocking collectives: none -> 75.1 us  [the longest x1 33.4 us: shards(): parts = lax.all_to_all(parts, 'member', 0, 0)]
    scatter-add x2 -> x0, other arithmetic: 51.6 us -> none  [picker(): jax.ops.segment_sum(selected, positions % block_len, num_segments=block_len)]
    select_n x2 -> x0, local copies, waits for them, and re-layouts: 9.94 us -> none  [picker(): jnp.where(keep_rows[:, None], shard_rows, jnp.zeros_like(shard_rows))]
    all_to_all x0 -> x2, waiting for transfers between devices: none -> 9.8 us  [the longest x1 7.13 us: shards(): lax.all_to_all(sent, 'group', 0, 0).reshape(groups * step, rows + hubs)]
    all_to_all x0 -> x2, starting transfers between devices: none -> 7.79 us  [the longest x1 4.18 us: shards(): lax.all_to_all(sent, 'group', 0, 0).reshape(groups * step, rows + hubs)]
  transfers between devices with their start and end apart: 3 -> 2, of which waited for: 3 -> 2; matrix products, arithmetic and copies ran while one was open for 2% -> 0% of each run, Pallas kernels for 0% -> 1%
where the time goes in v1:
time: 115 us; the launch traced here: 114 us
  blocking collectives  75.1 us (65%)
  local copies, waits for them, and re-layouts  11.9 us (10%)
  waiting for transfers between devices  9.8 us (9%)
  starting transfers between devices  7.79 us (7%)
  Pallas kernels  5.67 us (5%)
  other arithmetic  2.71 us (2%)
  between operations  1.47 us (1%)
    all_to_all x1, blocking collectives, shards(): parts = lax.all_to_all(parts, 'member', 0, 0)  33.4 us
    all_to_all x1, blocking collectives, shards(): got = lax.all_to_all(grads, 'group', 0, 0)  26.9 us
    all_to_all x1, blocking collectives, shards(): cut = lax.all_to_all(cut, 'group', 0, 0)  14.9 us
    unnamed x28, local copies, waits for them, and re-layouts  10.8 us
    all_to_all x1, waiting for transfers between devices, shards(): lax.all_to_all(sent, 'group', 0, 0).reshape(groups * step, rows + hubs)  7.13 us
    all_to_all x1, starting transfers between devices, shards(): lax.all_to_all(sent, 'group', 0, 0).reshape(groups * step, rows + hubs)  4.18 us
    all_to_all x1, starting transfers between devices, shards(): partner = lax.all_to_all(cut, 'group', 0, 0).reshape(groups * step, rows)  3.6 us
    all_to_all x1, waiting for transfers between devices, shards(): partner = lax.all_to_all(cut, 'group', 0, 0).reshape(groups * step, rows)  2.68 us
  transfers between devices with their start and end apart: 2, of which 2 were waited for; matrix products, arithmetic and copies ran while one was open for 0% of the time, Pallas kernels for 1%

profile of v1, /device:TPU:64, one launch (start us, length us, event | category | flops | bytes accessed | tf_op | source)
XLA Modules:
  0.0 114.5 jit_solution(188453826281971835)
XLA Ops:
  0.7 1.1 pad.4
  1.7 14.9 %all_to_all.25.rows = bf16[8,56,512]{2,1,0:T(8,128)(2,1)S(1)} all-to-all(bf16[8,56,512]{2,1,0:T(8,128)(2,1)S(1)} %bitcast.17), channel_id=1, replica_groups=mesh['group'=8,'member'=32] {'group'}, dimensions={0} | all-to-all | bytes 917504 | tf_op jit(solution)/shard_map/all_to_all | solution.py:156
  16.6 0.7 copy-done.2
  17.3 1.3 %shard_map.96 = bf16[8,56,512]{2,1,0:T(8,128)(2,1)} custom-call(s32[8]{0:T(128)S(1)} %copy-done.2, bf16[8,56,512]{2,1,0:T(8,128)(2,1)S(1)} %all_to_all.25.rows), custom_call_target="tpu_custom_call" | custom-call | bytes 917504 | tf_op jit(solution)/shard_map/pallas_call | solution.py:157
  18.6 3.6 %all-to-all-start.1 = ((bf16[8,56,512]{2,1,0:T(8,128)(2,1)}), bf16[8,56,512]{2,1,0:T(8,128)(2,1)S(1)}, u32[]{:S(2)}, u32[]{:S(2)}) async-start(bf16[8,56,512]{2,1,0:T(8,128)(2,1)} %shard_map.96), calls=%async_computation.1 | async-start | bytes 917504 | tf_op jit(solution)/shard_map/all_to_all | solution.py:160
  22.9 2.0 %copy-done.4 = f32[2112,400]{0,1:T(8,128)S(1)} copy-done((f32[2112,400]{0,1:T(8,128)S(1)}, f32[2112,400]{0,1:T(8,128)}, u32[]{:S(2)}) %copy-start.4) | copy-done | bytes 3379224
  24.9 0.9 shard_map.95
  25.8 1.7 %copy-done.8 = bf16[16,400,256]{2,1,0:T(8,128)(2,1)} copy-done((bf16[16,400,256]{2,1,0:T(8,128)(2,1)}, bf16[16,400,256]{2,1,0:T(8,128)(2,1)S(1)}, u32[]{:S(2)}) %copy-start.8) | copy-done | bytes 3276824
  27.5 2.7 %all-to-all-done.1 = bf16[8,56,512]{2,1,0:T(8,128)(2,1)S(1)} async-done(((bf16[8,56,512]{2,1,0:T(8,128)(2,1)}), bf16[8,56,512]{2,1,0:T(8,128)(2,1)S(1)}, u32[]{:S(2)}, u32[]{:S(2)}) %all-to-all-start.1) | async-done | bytes 458784 | tf_op jit(solution)/shard_map/all_to_all | solution.py:160
  30.2 1.9 %copy-done.9 = bf16[16,400,256]{2,1,0:T(8,128)(2,1)S(1)} copy-done((bf16[16,400,256]{2,1,0:T(8,128)(2,1)S(1)}, bf16[16,400,256]{2,1,0:T(8,128)(2,1)}, u32[]{:S(2)}) %copy-start.9) | copy-done | bytes 3276824
  32.1 1.5 %shard_map.97 = (bf16[16,400,256]{2,1,0:T(8,128)(2,1)S(1)}, bf16[16,256,256]{2,1,0:T(8,128)(2,1)S(1)}, bf16[8,56,640]{2,1,0:T(8,128)(2,1)S(1)}) custom-call(s32[1,1]{1,0:T(1,128)S(6)} %copy.10.count, bf16[16,400,256]{2,1,0:T(8,128)(2,1)S(1)} %copy-done.9, bf16[448,512]{1,0:T(8,128)(2,1)S(1)} %bitcast.14, bf16[400,128]{1,0:T(8,128)(2,1)S(1)} %bitcast.15, ...), custom_call_target="tpu_custom_call" | custom-call | flops 5872025600 | bytes 13107200 | tf_op jit(solution)/shard_map/pallas_call | solution.py:171
  33.6 1.7 %copy-done.10 = bf16[16,400,256]{2,1,0:T(8,128)(2,1)} copy-done((bf16[16,400,256]{2,1,0:T(8,128)(2,1)}, bf16[16,400,256]{2,1,0:T(8,128)(2,1)S(1)}, u32[]{:S(2)}) %copy-start.10) | copy-done | bytes 3276824
  35.3 26.9 %all_to_all.26.back = bf16[8,56,640]{2,1,0:T(8,128)(2,1)S(1)} all-to-all(bf16[8,56,640]{2,1,0:T(8,128)(2,1)S(1)} %get-tuple-element.11), channel_id=1, replica_groups=mesh['group'=8,'member'=32] {'group'}, dimensions={0} | all-to-all | bytes 1146880 | tf_op jit(solution)/shard_map/all_to_all | solution.py:192
  62.1 0.1 broadcast_in_dim.2
  62.2 33.4 %all_to_all.27.hub = bf16[32,56,128]{2,1,0:T(8,128)(2,1)S(1)} all-to-all(bf16[32,56,128]{2,1,0:T(8,128)(2,1)S(1)} %broadcast_in_dim.2), channel_id=1, replica_groups=mesh['group'=8,'member'=32] {'member'}, dimensions={0} | all-to-all | bytes 917504 | tf_op jit(solution)/shard_map/all_to_all | solution.py:195
  95.6 1.5 %shard_map.99 = bf16[8,56,640]{2,1,0:T(8,128)(2,1)} custom-call(s32[8]{0:T(128)S(1)} %copy-done.3, bf16[8,56,640]{2,1,0:T(8,128)(2,1)S(1)} %all_to_all.26.back, bf16[32,56,128]{2,1,0:T(8,128)(2,1)S(1)} %all_to_all.27.hub), custom_call_target="tpu_custom_call" | custom-call | bytes 1146880 | tf_op jit(solution)/shard_map/pallas_call | solution.py:196
  97.1 4.2 %all-to-all-start.4 = ((bf16[8,56,640]{2,1,0:T(8,128)(2,1)}), bf16[8,56,640]{2,1,0:T(8,128)(2,1)}, u32[]{:S(2)}, u32[]{:S(2)}) async-start(bf16[8,56,640]{2,1,0:T(8,128)(2,1)} %shard_map.99), calls=%async_computation.4 | async-start | bytes 1146880 | tf_op jit(solution)/shard_map/all_to_all | solution.py:199
  101.3 1.9 %copy-done.11 = bf16[16,400,256]{2,1,0:T(8,128)(2,1)S(1)} copy-done((bf16[16,400,256]{2,1,0:T(8,128)(2,1)S(1)}, bf16[16,400,256]{2,1,0:T(8,128)(2,1)}, u32[]{:S(2)}) %copy-start.11) | copy-done | bytes 3276824
  103.2 0.9 copy-done.13
  104.2 0.5 shard_map.98
  104.7 7.1 %all-to-all-done.4 = bf16[8,56,640]{2,1,0:T(8,128)(2,1)} async-done(((bf16[8,56,640]{2,1,0:T(8,128)(2,1)}), bf16[8,56,640]{2,1,0:T(8,128)(2,1)}, u32[]{:S(2)}, u32[]{:S(2)}) %all-to-all-start.4) | async-done | bytes 573472 | tf_op jit(solution)/shard_map/all_to_all | solution.py:199
  111.8 1.1 slice_convert_fusion
  112.9 0.7 fusion.6
  113.6 0.9 fusion.3
  (22 shorter events, 0.1 us)
Async XLA Ops:
  0.6 22.3 %copy-start = (bf16[512,400]{0,1:T(8,128)(2,1)S(1)}, bf16[512,400]{0,1:T(8,128)(2,1)}, u32[]{:S(2)}) copy-start(bf16[512,400]{0,1:T(8,128)(2,1)} %param.8) | copy-start | bytes 1228804
  0.6 22.3 %copy-start.6 = (s32[16,256]{1,0:T(8,128)S(1)}, s32[16,256]{1,0:T(8,128)}, u32[]{:S(2)}) copy-start(s32[16,256]{1,0:T(8,128)} %heads.3) | copy-start | bytes 49156
  0.6 22.3 %copy-start.7 = (s32[16]{0:T(128)S(1)}, s32[16]{0:T(128)}, u32[]{:S(2)}) copy-start(s32[16]{0:T(128)} %rel_ids.1) | copy-start | bytes 196
  16.6 0.7 copy-start.2
  18.6 11.6 %copy-start.5 = (s32[16,256]{1,0:T(8,128)S(1)}, s32[16,256]{1,0:T(8,128)}, u32[]{:S(2)}) copy-start(s32[16,256]{1,0:T(8,128)} %tails.1) | copy-start | bytes 49156
  18.6 11.6 %all-to-all-start.1 = ((bf16[8,56,512]{2,1,0:T(8,128)(2,1)}), bf16[8,56,512]{2,1,0:T(8,128)(2,1)S(1)}, u32[]{:S(2)}, u32[]{:S(2)}) async-start(bf16[8,56,512]{2,1,0:T(8,128)(2,1)} %shard_map.96), calls=%async_computation.1 | async-start | bytes 917504 | tf_op jit(solution)/shard_map/all_to_all | solution.py:160
  22.2 8.0 %copy-start.1 = (bf16[128,400]{0,1:T(8,128)(2,1)S(1)}, bf16[128,400]{0,1:T(8,128)(2,1)}, u32[]{:S(2)}) copy-start(bf16[128,400]{0,1:T(8,128)(2,1)} %param.9) | copy-start | bytes 307204
  22.9 2.0 %copy-start.4 = (f32[2112,400]{0,1:T(8,128)S(1)}, f32[2112,400]{0,1:T(8,128)}, u32[]{:S(2)}) copy-start(f32[2112,400]{0,1:T(8,128)} %param.10) | copy-start | bytes 10137604
  25.8 1.7 %copy-start.8 = (bf16[16,400,256]{2,1,0:T(8,128)(2,1)}, bf16[16,400,256]{2,1,0:T(8,128)(2,1)S(1)}, u32[]{:S(2)}) copy-start(bf16[16,400,256]{2,1,0:T(8,128)(2,1)S(1)} %get-tuple-element.7.query) | copy-start | bytes 9830404
  27.5 6.1 %copy-start.12 = (f32[400,128]{1,0:T(8,128)}, f32[400,128]{1,0:T(8,128)S(1)}, u32[]{:S(2)}) copy-start(f32[400,128]{1,0:T(8,128)S(1)} %get-tuple-element.10.weights) | copy-start | bytes 614404
  30.2 1.9 %copy-start.9 = (bf16[16,400,256]{2,1,0:T(8,128)(2,1)S(1)}, bf16[16,400,256]{2,1,0:T(8,128)(2,1)}, u32[]{:S(2)}) copy-start(bf16[16,400,256]{2,1,0:T(8,128)(2,1)} %copy-done.8) | copy-start | bytes 9830404
  32.1 63.6 %copy-start.3 = (s32[8]{0:T(128)S(1)}, s32[8]{0:T(128)}, u32[]{:S(2)}) copy-start(s32[8]{0:T(128)} %matching.3) | copy-start | bytes 100
  33.6 1.7 %copy-start.10 = (bf16[16,400,256]{2,1,0:T(8,128)(2,1)}, bf16[16,400,256]{2,1,0:T(8,128)(2,1)S(1)}, u32[]{:S(2)}) copy-start(bf16[16,400,256]{2,1,0:T(8,128)(2,1)S(1)} %get-tuple-element.8.pick) | copy-start | bytes 9830404
  97.1 14.7 %all-to-all-start.4 = ((bf16[8,56,640]{2,1,0:T(8,128)(2,1)}), bf16[8,56,640]{2,1,0:T(8,128)(2,1)}, u32[]{:S(2)}, u32[]{:S(2)}) async-start(bf16[8,56,640]{2,1,0:T(8,128)(2,1)} %shard_map.99), calls=%async_computation.4 | async-start | bytes 1146880 | tf_op jit(solution)/shard_map/all_to_all | solution.py:199
  101.3 1.9 %copy-start.11 = (bf16[16,400,256]{2,1,0:T(8,128)(2,1)S(1)}, bf16[16,400,256]{2,1,0:T(8,128)(2,1)}, u32[]{:S(2)}) copy-start(bf16[16,400,256]{2,1,0:T(8,128)(2,1)} %copy-done.10) | copy-start | bytes 9830404
  103.2 0.9 copy-start.13

commit v2 on v1

v2 whole, which is shorter than its diff:
```python
import jax
import jax.numpy as jnp
from jax import lax
from jax.experimental import pallas as pl
from jax.experimental.pallas import tpu as pltpu
from jax.sharding import PartitionSpec as P

learn_rate = 0.1
BF = jnp.bfloat16
F32 = jnp.float32
LANES = 128
VMEM = pl.BlockSpec(memory_space=pltpu.VMEM)
SMEM = pl.BlockSpec(memory_space=pltpu.SMEM)
HBM = pl.BlockSpec(memory_space=pltpu.HBM)
DMA = pltpu.SemaphoreType.DMA


def hot(ids, rows):
    row = lax.broadcasted_iota(jnp.int32, (rows, ids.shape[1]), 0)
    return jnp.where(row == ids, 1.0, 0.0).astype(BF)


def pair_ids(ids_ref, pair):
    return jnp.concatenate([ids_ref[pl.ds(2 * pair, 1), :], ids_ref[pl.ds(2 * pair + 1, 1), :]], axis=1)


def pick_lane(block, lane):
    lanes = lax.broadcasted_iota(jnp.int32, block.shape, 1)
    return jnp.sum(jnp.where(lanes == lane, block, 0.0), axis=1, keepdims=True)


def dot_nn(a, b):
    return lax.dot_general(a, b, (((1,), (0,)), ((), ())), preferred_element_type=F32)


def dot_nt(a, b):
    return lax.dot_general(a, b, (((1,), (1,)), ((), ())), preferred_element_type=F32)


def dot_tn(a, b):
    return lax.dot_general(a, b, (((0,), (0,)), ((), ())), preferred_element_type=F32)


def query_kernel(count, rel_ids, ent, rel, heads, query, weights, block, out, sems):
    half = ent.shape[0] // 2
    edges = query.shape[2]
    whole = rel.shape[1] // LANES
    rest = rel.shape[1] - whole * LANES
    live = count[0, 0]
    pairs = (live + 1) // 2
    weights[...] = jnp.zeros_like(weights)
    block[...] = jnp.zeros_like(block)

    def copy(pair):
        slot = pair % 2
        return pltpu.make_async_copy(out.at[slot], query.at[pl.ds(2 * pair, 2)], sems.at[slot])

    @pl.loop(0, pairs)
    def _(pair):
        @pl.when(pair >= 2)
        def _():
            copy(pair - 2).wait()

        for k in range(2):
            at = rel_ids[2 * pair + k] // LANES

            @pl.when(at < whole)
            def _():
                block[k] = rel[:, pl.ds(pl.multiple_of(at * LANES, LANES), LANES)]

            if rest:

                @pl.when(at >= whole)
                def _():
                    block[k, :, :rest] = rel[:, whole * LANES :]

        head = dot_nn(ent[...], hot(pair_ids(heads, pair), ent.shape[1]))
        for k in range(2):
            tile = 2 * pair + k
            rid = rel_ids[tile]
            w = pick_lane(block[k], rid - rid // LANES * LANES)
            w = jnp.where(tile < live, w, 0.0)
            lanes = lax.broadcasted_iota(jnp.int32, weights.shape, 1)
            weights[...] = jnp.where(lanes == tile, w, weights[...])
            hr = head[:half, k * edges : (k + 1) * edges]
            hi = head[half:, k * edges : (k + 1) * edges]
            wr, wi = w[:half], w[half:]
            out[pair % 2, k] = jnp.concatenate(
                [hr * wr - hi * wi, hr * wi + hi * wr], axis=0
            ).astype(BF)
        copy(pair).start()

    @pl.when(pairs >= 2)
    def _():
        copy(pairs - 2).wait()

    copy(pairs - 1).wait()


def tail_kernel(count, query, partner, hub, tails, pick, diff, grads, table, acc, qin, pout, dout, qsem, psem, dsem):
    dim, rows = hub.shape[0], partner.shape[1]
    edges = tails.shape[1]
    live = count[0, 0]
    pairs = (live + 1) // 2

    def fetch(pair):
        slot = pair % 2
        return pltpu.make_async_copy(query.at[pl.ds(2 * pair, 2)], qin.at[slot], qsem.at[slot])

    def put_pick(pair):
        slot = pair % 2
        return pltpu.make_async_copy(pout.at[slot], pick.at[pair], psem.at[slot])

    def put_diff(pair):
        slot = pair % 2
        return pltpu.make_async_copy(dout.at[slot], diff.at[pl.ds(2 * pair, 2)], dsem.at[slot])

    fetch(0).start()
    table[:, :rows] = partner[:dim]
    table[:, rows:] = hub[...]
    acc[...] = jnp.zeros_like(acc)
    eye = lax.broadcasted_iota(jnp.int32, (edges, edges), 0) == lax.broadcasted_iota(
        jnp.int32, (edges, edges), 1
    )

    @pl.loop(0, pairs)
    def _(pair):
        slot = pair % 2
        fetch(pair).wait()

        @pl.when(pair + 1 < pairs)
        def _():
            fetch(pair + 1).start()

        @pl.when(pair >= 2)
        def _():
            put_pick(pair - 2).wait()
            put_diff(pair - 2).wait()

        tail_hot = hot(pair_ids(tails, pair), table.shape[1])
        both = dot_nn(table[...], tail_hot).astype(BF)
        pout[slot] = both
        d_tails = []
        for k in range(2):
            q = qin[slot, k]
            tail = both[:, k * edges : (k + 1) * edges]
            scores = dot_tn(tail, q)
            top = jnp.max(scores, axis=0, keepdims=True)
            expo = jnp.exp(scores - top)
            probs = expo * (1.0 / jnp.sum(expo, axis=0, keepdims=True))
            d = jnp.where(eye, probs - 1.0, probs)
            if k:
                d = jnp.where(2 * pair + 1 < live, d, 0.0)
            d = d.astype(BF)
            dout[slot, k] = d
            d_tails.append(dot_nt(q, d).astype(BF))
        acc[...] += dot_nt(jnp.concatenate(d_tails, axis=1), tail_hot)
        put_pick(pair).start()
        put_diff(pair).start()

    chunks, step = grads.shape[0], grads.shape[1]
    for c in range(chunks):
        n = min(step, dim - c * step)
        grads[c, :n] = acc[c * step : c * step + n].astype(BF)
        if n < step:
            grads[c, n:] = jnp.zeros((step - n, grads.shape[2]), BF)

    @pl.when(pairs >= 2)
    def _():
        put_pick(pairs - 2).wait()
        put_diff(pairs - 2).wait()

    put_pick(pairs - 1).wait()
    put_diff(pairs - 1).wait()


def head_kernel(count, pick, diff, weights, heads, acc, pin, din, psem, dsem):
    half = acc.shape[0] // 2
    edges = heads.shape[1]
    live = count[0, 0]
    pairs = (live + 1) // 2

    def get_pick(pair):
        slot = pair % 2
        return pltpu.make_async_copy(pick.at[pair], pin.at[slot], psem.at[slot])

    def get_diff(pair):
        slot = pair % 2
        return pltpu.make_async_copy(diff.at[pl.ds(2 * pair, 2)], din.at[slot], dsem.at[slot])

    get_pick(0).start()
    get_diff(0).start()
    acc[...] = jnp.zeros_like(acc)

    @pl.loop(0, pairs)
    def _(pair):
        slot = pair % 2
        get_pick(pair).wait()
        get_diff(pair).wait()

        @pl.when(pair + 1 < pairs)
        def _():
            get_pick(pair + 1).start()
            get_diff(pair + 1).start()

        d_heads = []
        for k in range(2):
            d_query = dot_nn(pin[slot, :, k * edges : (k + 1) * edges], din[slot, k])
            w = pick_lane(weights[...], 2 * pair + k)
            dr, di = d_query[:half], d_query[half:]
            wr, wi = w[:half], w[half:]
            d_heads.append(
                jnp.concatenate([dr * wr + di * wi, di * wr - dr * wi], axis=0).astype(BF)
            )
        head_hot = hot(pair_ids(heads, pair), acc.shape[1])
        acc[...] += dot_nt(jnp.concatenate(d_heads, axis=1), head_hot)


def reorder_kernel(matching, rows, out):
    for g in range(out.shape[0]):
        out[g] = rows[matching[g]]


def return_kernel(matching, back, hub, out):
    rows = out.shape[2] - hub.shape[2]
    total = hub[0].astype(F32)
    for m in range(1, hub.shape[0]):
        total += hub[m].astype(F32)
    total = total.astype(BF)
    for g in range(out.shape[0]):
        out[matching[g], :, :rows] = back[g, :, :rows]
        out[g, :, rows:] = total


def update_kernel(ent, hub, head_acc, last, new_ent, new_hub):
    dim, rows = ent.shape
    step = last.shape[1]
    for c in range(last.shape[0]):
        n = min(step, dim - c * step)
        at = slice(c * step, c * step + n)
        got = last[c, :n].astype(F32)
        new_ent[at] = (ent[at].astype(F32) - learn_rate * (head_acc[at] + got[:, :rows])).astype(BF)
        new_hub[at] = (hub[at].astype(F32) - learn_rate * got[:, rows:]).astype(BF)


def call(kernel, out_shape, in_specs, out_specs, flops, moved, scratch=(), exps=0, vmem=32):
    return pl.pallas_call(
        kernel,
        out_shape=out_shape,
        in_specs=in_specs,
        out_specs=out_specs,
        scratch_shapes=scratch,
        compiler_params=pltpu.CompilerParams(vmem_limit_bytes=vmem * 1024 * 1024),
        cost_estimate=pl.CostEstimate(flops=flops, bytes_accessed=moved, transcendentals=exps),
    )


shape = jax.ShapeDtypeStruct


def run_query(tile_count, tile_rel, ent, rel, head_index):
    dim, rows = ent.shape
    tiles, edges = head_index.shape
    return call(
        query_kernel,
        [shape((tiles, dim, edges), BF), shape((dim, LANES), F32)],
        [SMEM, SMEM, VMEM, VMEM, VMEM],
        [HBM, VMEM],
        2 * tiles * edges * dim * rows,
        8 * rel.size,
        [pltpu.VMEM((2, dim, LANES), F32), pltpu.VMEM((2, 2, dim, edges), BF), DMA((2,))],
        vmem=58,
    )(tile_count, tile_rel, ent, rel, head_index)


def run_tail(tile_count, query, partner, hub, tail_index, groups, step):
    tiles, dim, edges = query.shape
    rows, hubs = partner.shape[1], hub.shape[1]
    return call(
        tail_kernel,
        [
            shape((tiles // 2, dim, 2 * edges), BF),
            shape((tiles, edges, edges), BF),
            shape((groups, step, rows + hubs), BF),
        ],
        [SMEM, HBM, VMEM, VMEM, VMEM],
        [HBM, HBM, VMEM],
        4 * tiles * edges * dim * (rows + hubs + edges),
        8 * tiles * dim * edges,
        [
            pltpu.VMEM((dim, rows + hubs), BF),
            pltpu.VMEM((dim, rows + hubs), F32),
            pltpu.VMEM((2, 2, dim, edges), BF),
            pltpu.VMEM((2, dim, 2 * edges), BF),
            pltpu.VMEM((2, 2, edges, edges), BF),
            DMA((2,)),
            DMA((2,)),
            DMA((2,)),
        ],
        tiles * edges * edges,
        vmem=61,
    )(tile_count, query, partner, hub, tail_index)


def run_head(tile_count, pick, diff, weights, head_index, rows):
    pairs, dim, wide = pick.shape
    edges = wide // 2
    return call(
        head_kernel,
        shape((dim, rows), F32),
        [SMEM, HBM, HBM, VMEM, VMEM],
        VMEM,
        4 * pairs * edges * dim * (rows + edges),
        12 * pairs * dim * edges,
        [
            pltpu.VMEM((2, dim, wide), BF),
            pltpu.VMEM((2, 2, edges, edges), BF),
            DMA((2,)),
            DMA((2,)),
        ],
        vmem=61,
    )(tile_count, pick, diff, weights, head_index)


def make(groups, members):
    def shards(entities, hub_rows, relations, matching, head_index, tail_index, tile_rel, tile_count):
        ent, hub, rel = entities.T, hub_rows.T, relations.T
        dim, rows = ent.shape
        hubs = hub.shape[1]
        step = -(-dim // (8 * groups)) * 8

        cut = jnp.pad(ent, ((0, groups * step - dim), (0, 0))).reshape(groups, step, rows)
        cut = lax.all_to_all(cut, "group", 0, 0)
        query, weights = run_query(tile_count, tile_rel, ent, rel, head_index)
        cut, query, weights = lax.optimization_barrier((cut, query, weights))
        cut = call(reorder_kernel, shape(cut.shape, BF), [SMEM, VMEM], VMEM, 0, 4 * cut.size)(
            matching, cut
        )
        partner = lax.all_to_all(cut, "group", 0, 0).reshape(groups * step, rows)
        pick, diff, grads = run_tail(tile_count, query, partner, hub, tail_index, groups, step)

        got = lax.all_to_all(grads, "group", 0, 0)
        got, pick, diff = lax.optimization_barrier((got, pick, diff))
        part = jnp.sum(got[:, :, rows:].astype(F32), axis=0).astype(BF)
        parts = jnp.broadcast_to(part[None], (members,) + part.shape)
        parts = lax.all_to_all(parts, "member", 0, 0)
        head_acc = run_head(tile_count, pick, diff, weights, head_index, rows)
        parts, head_acc = lax.optimization_barrier((parts, head_acc))
        sent = call(
            return_kernel, shape(got.shape, BF), [SMEM, VMEM, VMEM], VMEM, 0, 4 * got.size
        )(matching, got, parts)
        last = lax.all_to_all(sent, "group", 0, 0)
        new_ent, new_hub = call(
            update_kernel,
            [shape((dim, rows), BF), shape((dim, hubs), BF)],
            [VMEM, VMEM, VMEM, VMEM],
            [VMEM, VMEM],
            0,
            8 * dim * rows,
        )(ent, hub, head_acc, last)
        return (new_ent.T, new_hub.T)

    return shards


def solution(mesh):
    placed = (
        P(("group", "member"), None),
        P(),
        P(),
        P(),
        P(("group", "member"), None),
        P(("group", "member"), None),
        P(("group", "member")),
        P("group", "member"),
    )
    return jax.shard_map(
        make(mesh.shape["group"], mesh.shape["member"]),
        mesh=mesh,
        in_specs=placed,
        out_specs=(P(("group", "member"), None), P()),
        check_vma=False,
    )
```

time: 115 us -> 108 us (0.939); the launches traced: 114 us -> 106 us
  blocking collectives: 75.1 us -> 48.5 us
  Pallas kernels: 5.67 us -> 22.3 us
  starting transfers between devices: 7.79 us -> 17.4 us
  local copies, waits for them, and re-layouts: 11.9 us -> 2.66 us
  waiting for transfers between devices: 9.8 us -> 13.7 us
  other arithmetic: 2.71 us -> 0.02 us
    all_to_all x2, blocking collectives: 48.3 us -> 27 us  [the longest x1 13.9 us: shards(): last = lax.all_to_all(sent, 'group', 0, 0)]
    pallas_call x5 -> x6, Pallas kernels: 5.67 us -> 22.3 us  [the longest x1 8.99 us: run_tail(): call(tail_kernel, [shape((tiles // 2, dim, 2 * edges), BF), shape((tiles,...]
    unnamed x28 -> x8, local copies, waits for them, and re-layouts: 10.8 us -> 0.02 us
    all_to_all x2, starting transfers between devices: 7.79 us -> 17.4 us  [the longest x1 11.7 us: shards(): parts = lax.all_to_all(parts, 'member', 0, 0)]
    all_to_all x1, blocking collectives: 26.9 us -> 21.5 us  [shards(): got = lax.all_to_all(grads, 'group', 0, 0)]
    all_to_all x2, waiting for transfers between devices: 9.8 us -> 13.7 us  [the longest x1 10.6 us: shards(): parts = lax.all_to_all(parts, 'member', 0, 0)]
    transpose x2 -> x0, other arithmetic: 1.58 us -> none  [shards(): return (new_entities.T, new_hub.T)]
  transfers between devices with their start and end apart: 2 -> 2, of which waited for: 2 -> 2; matrix products, arithmetic and copies ran while one was open for 0% -> 0% of each run, Pallas kernels for 1% -> 10%
where the time goes in v2:
time: 108 us; the launch traced here: 106 us
  blocking collectives  48.5 us (45%)
  Pallas kernels  22.3 us (21%)
  starting transfers between devices  17.4 us (16%)
  waiting for transfers between devices  13.7 us (13%)
  local copies, waits for them, and re-layouts  2.66 us (2%)
  between operations  1.37 us (1%)
    all_to_all x1, blocking collectives, shards(): got = lax.all_to_all(grads, 'group', 0, 0)  21.5 us
    all_to_all x1, blocking collectives, shards(): last = lax.all_to_all(sent, 'group', 0, 0)  13.9 us
    all_to_all x1, blocking collectives, shards(): partner = lax.all_to_all(cut, 'group', 0, 0).reshape(groups * step, rows)  13.1 us
    all_to_all x1, starting transfers between devices, shards(): parts = lax.all_to_all(parts, 'member', 0, 0)  11.7 us
    all_to_all x1, waiting for transfers between devices, shards(): parts = lax.all_to_all(parts, 'member', 0, 0)  10.6 us
    pallas_call x1, Pallas kernels, run_tail(): call(tail_kernel, [shape((tiles // 2, dim, 2 * edges), BF), shape((tiles,...  8.99 us
    pallas_call x1, Pallas kernels, run_head(): call(head_kernel, shape((dim, rows), F32), [SMEM, HBM, HBM, VMEM, VMEM],...  5.82 us
    all_to_all x1, starting transfers between devices, shards(): cut = lax.all_to_all(cut, 'group', 0, 0)  5.65 us
  transfers between devices with their start and end apart: 2, of which 2 were waited for; matrix products, arithmetic and copies ran while one was open for 0% of the time, Pallas kernels for 10%

profile of v2, /device:TPU:64, one launch (start us, length us, event | category | flops | bytes accessed | tf_op | source)
XLA Modules:
  0.0 105.9 jit_solution(9003243810308548009)
XLA Ops:
  0.6 1.8 %pad.4 = bf16[448,512]{1,0:T(8,128)(2,1)} pad(bf16[400,512]{1,0:T(8,128)(2,1)} %bitcast.7, bf16[]{:T(256)} %constant.4.clone.1), padding=0_48x0_0 | pad | bytes 868354 | tf_op jit(solution)/shard_map/jit(_pad)/pad | solution.py:332
  2.4 5.7 %all-to-all-start = ((bf16[8,56,512]{2,1,0:T(8,128)(2,1)}), bf16[8,56,512]{2,1,0:T(8,128)(2,1)S(1)}, u32[]{:S(2)}, u32[]{:S(2)}) async-start(bf16[8,56,512]{2,1,0:T(8,128)(2,1)} %bitcast.2), calls=%async_computation | async-start | bytes 917504 | tf_op jit(solution)/shard_map/all_to_all | solution.py:333
  8.1 0.0 copy-start.3
  8.8 5.3 %shard_map.95 = (bf16[16,400,256]{2,1,0:T(8,128)(2,1)}, f32[400,128]{1,0:T(8,128)}) custom-call(s32[1,1]{1,0:T(1,128)S(6)} %copy.10.count, s32[16]{0:T(128)} %rel_ids.1, bf16[400,512]{1,0:T(8,128)(2,1)} %bitcast.8, f32[400,2112]{1,0:T(8,128)} %bitcast.13, s32[16,256]{1,0:T(8,128)} %heads.3), custom_call_target="tpu_custom_call" | custom-call | flops 1677721600 | bytes 6758400 | tf_op jit(solution)/shard_map/pallas_call | solution.py:264
  14.1 3.1 %all-to-all-done.rows = bf16[8,56,512]{2,1,0:T(8,128)(2,1)S(1)} async-done(((bf16[8,56,512]{2,1,0:T(8,128)(2,1)}), bf16[8,56,512]{2,1,0:T(8,128)(2,1)S(1)}, u32[]{:S(2)}, u32[]{:S(2)}) %all-to-all-start) | async-done | bytes 458784 | tf_op jit(solution)/shard_map/all_to_all | solution.py:333
  17.1 0.0 copy-done.3
  17.1 0.6 shard_map.96
  17.7 13.1 %all_to_all.25 = bf16[8,56,512]{2,1,0:T(8,128)(2,1)} all-to-all(bf16[8,56,512]{2,1,0:T(8,128)(2,1)S(1)} %shard_map.96), channel_id=1, replica_groups=mesh['group'=8,'member'=32] {'group'}, dimensions={0} | all-to-all | bytes 917504 | tf_op jit(solution)/shard_map/all_to_all | solution.py:339
  30.8 9.0 %shard_map.97 = (bf16[8,400,512]{2,1,0:T(8,128)(2,1)}, bf16[16,256,256]{2,1,0:T(8,128)(2,1)}, bf16[8,56,640]{2,1,0:T(8,128)(2,1)}) custom-call(s32[1,1]{1,0:T(1,128)S(6)} %copy.10.count, bf16[16,400,256]{2,1,0:T(8,128)(2,1)} %get-tuple-element.19.query, bf16[448,512]{1,0:T(8,128)(2,1)} %bitcast.12, bf16[400,128]{1,0:T(8,128)(2,1)} %bitcast.10, s32[16,256]{1,0:T(8,128)} %tails.1), custom_call_target="tpu_custom_call" | custom-call | flops 5872025600 | bytes 13107200 | tf_op jit(solution)/shard_map/pallas_call | solution.py:279
  39.8 21.5 %all_to_all.26.back = bf16[8,56,640]{2,1,0:T(8,128)(2,1)S(1)} all-to-all(bf16[8,56,640]{2,1,0:T(8,128)(2,1)} %get-tuple-element.21), channel_id=1, replica_groups=mesh['group'=8,'member'=32] {'group'}, dimensions={0} | all-to-all | bytes 1146880 | tf_op jit(solution)/shard_map/all_to_all | solution.py:342
  61.4 0.8 broadcast_in_dim.2
  62.2 11.7 %all-to-all-start.3 = ((bf16[32,56,128]{2,1,0:T(8,128)(2,1)}), bf16[32,56,128]{2,1,0:T(8,128)(2,1)S(1)}, u32[]{:S(2)}, u32[]{:S(2)}) async-start(bf16[32,56,128]{2,1,0:T(8,128)(2,1)} %broadcast_in_dim.2), calls=%async_computation.3 | async-start | bytes 917504 | tf_op jit(solution)/shard_map/all_to_all | solution.py:346
  74.0 0.0 copy-start
  74.0 0.0 copy-start.2
  74.0 5.8 %shard_map.98.head_acc = f32[400,512]{1,0:T(8,128)} custom-call(s32[1,1]{1,0:T(1,128)S(6)} %copy.10.count, bf16[8,400,512]{2,1,0:T(8,128)(2,1)} %get-tuple-element.25.pick, bf16[16,256,256]{2,1,0:T(8,128)(2,1)} %get-tuple-element.26.diff, f32[400,128]{1,0:T(8,128)} %get-tuple-element.27.weights, s32[16,256]{1,0:T(8,128)} %heads.3), custom_call_target="tpu_custom_call" | custom-call | flops 2516582400 | bytes 9830400 | tf_op jit(solution)/shard_map/pallas_call | solution.py:308
  79.8 0.0 copy-start.1
  79.8 10.6 %all-to-all-done.3.hub = bf16[32,56,128]{2,1,0:T(8,128)(2,1)S(1)} async-done(((bf16[32,56,128]{2,1,0:T(8,128)(2,1)}), bf16[32,56,128]{2,1,0:T(8,128)(2,1)S(1)}, u32[]{:S(2)}, u32[]{:S(2)}) %all-to-all-start.3) | async-done | bytes 458784 | tf_op jit(solution)/shard_map/all_to_all | solution.py:346
  90.4 0.7 shard_map.99
  91.1 13.9 %all_to_all.27.last = bf16[8,56,640]{2,1,0:T(8,128)(2,1)S(1)} all-to-all(bf16[8,56,640]{2,1,0:T(8,128)(2,1)S(1)} %shard_map.99), channel_id=1, replica_groups=mesh['group'=8,'member'=32] {'group'}, dimensions={0} | all-to-all | bytes 1146880 | tf_op jit(solution)/shard_map/all_to_all | solution.py:352
  104.9 0.0 copy-done
  104.9 0.0 copy-done.2
  104.9 0.0 copy-done.1
  104.9 1.0 shard_map.100
  (1 shorter events, 0.0 us)
Async XLA Ops:
  2.4 14.7 %all-to-all-start = ((bf16[8,56,512]{2,1,0:T(8,128)(2,1)}), bf16[8,56,512]{2,1,0:T(8,128)(2,1)S(1)}, u32[]{:S(2)}, u32[]{:S(2)}) async-start(bf16[8,56,512]{2,1,0:T(8,128)(2,1)} %bitcast.2), calls=%async_computation | async-start | bytes 917504 | tf_op jit(solution)/shard_map/all_to_all | solution.py:333
  8.1 9.1 %copy-start.3 = (s32[8]{0:T(128)S(1)}, s32[8]{0:T(128)}, u32[]{:S(2)}) copy-start(s32[8]{0:T(128)} %matching.3) | copy-start | bytes 100
  62.2 28.2 %all-to-all-start.3 = ((bf16[32,56,128]{2,1,0:T(8,128)(2,1)}), bf16[32,56,128]{2,1,0:T(8,128)(2,1)S(1)}, u32[]{:S(2)}, u32[]{:S(2)}) async-start(bf16[32,56,128]{2,1,0:T(8,128)(2,1)} %broadcast_in_dim.2), calls=%async_computation.3 | async-start | bytes 917504 | tf_op jit(solution)/shard_map/all_to_all | solution.py:346
  74.0 31.0 %copy-start = (bf16[512,400]{0,1:T(8,128)(2,1)S(1)}, bf16[512,400]{0,1:T(8,128)(2,1)}, u32[]{:S(2)}) copy-start(bf16[512,400]{0,1:T(8,128)(2,1)} %param.8) | copy-start | bytes 1228804
  74.0 30.9 %copy-start.2 = (bf16[128,400]{0,1:T(8,128)(2,1)S(1)}, bf16[128,400]{0,1:T(8,128)(2,1)}, u32[]{:S(2)}) copy-start(bf16[128,400]{0,1:T(8,128)(2,1)} %param.9) | copy-start | bytes 307204
  79.8 25.1 %copy-start.1 = (f32[400,512]{1,0:T(8,128)S(1)}, f32[400,512]{1,0:T(8,128)}, u32[]{:S(2)}) copy-start(f32[400,512]{1,0:T(8,128)} %shard_map.98.head_acc) | copy-start | bytes 2457604

commit v3 on v2

v3 whole, which is shorter than its diff:
```python
import jax
import jax.numpy as jnp
from jax import lax
from jax.experimental import pallas as pl
from jax.experimental.pallas import tpu as pltpu
from jax.sharding import PartitionSpec as P

learn_rate = 0.1
BF = jnp.bfloat16
F32 = jnp.float32
LANES = 128
VMEM = pl.BlockSpec(memory_space=pltpu.VMEM)
SMEM = pl.BlockSpec(memory_space=pltpu.SMEM)
HBM = pl.BlockSpec(memory_space=pltpu.HBM)
DMA = pltpu.SemaphoreType.DMA


def hot(ids, rows):
    row = lax.broadcasted_iota(jnp.int32, (rows, ids.shape[1]), 0)
    return jnp.where(row == ids, 1.0, 0.0).astype(BF)


def pair_ids(ids_ref, pair):
    return jnp.concatenate([ids_ref[pl.ds(2 * pair, 1), :], ids_ref[pl.ds(2 * pair + 1, 1), :]], axis=1)


def pick_lane(block, lane):
    lanes = lax.broadcasted_iota(jnp.int32, block.shape, 1)
    return jnp.sum(jnp.where(lanes == lane, block, 0.0), axis=1, keepdims=True)


def dot_nn(a, b):
    return lax.dot_general(a, b, (((1,), (0,)), ((), ())), preferred_element_type=F32)


def dot_nt(a, b):
    return lax.dot_general(a, b, (((1,), (1,)), ((), ())), preferred_element_type=F32)


def dot_tn(a, b):
    return lax.dot_general(a, b, (((0,), (0,)), ((), ())), preferred_element_type=F32)


def rotate_pair(pair, live, ent, heads, weights, out):
    half, edges = ent.shape[0] // 2, heads.shape[1]
    head = dot_nn(ent[...], hot(pair_ids(heads, pair), ent.shape[1]))
    for k in range(2):
        w = pick_lane(weights[...], 2 * pair + k)
        hr = head[:half, k * edges : (k + 1) * edges]
        hi = head[half:, k * edges : (k + 1) * edges]
        wr, wi = w[:half], w[half:]
        out[k] = jnp.concatenate([hr * wr - hi * wi, hr * wi + hi * wr], axis=0).astype(BF)


def first_kernel(count, rel_ids, ent, rel, heads, query, weights, table, block, out, rel_sem, sem):
    live = count[0, 0]
    whole = rel.shape[1] // LANES
    rest = rel.shape[1] - whole * LANES
    load = pltpu.make_async_copy(rel, table, rel_sem)
    load.start()
    weights[...] = jnp.zeros_like(weights)
    block[...] = jnp.zeros_like(block)
    load.wait()

    @pl.loop(0, (live + 1) // 2)
    def _(pair):
        for k in range(2):
            at = rel_ids[2 * pair + k] // LANES

            @pl.when(at < whole)
            def _():
                block[k] = table[:, pl.ds(pl.multiple_of(at * LANES, LANES), LANES)]

            if rest:

                @pl.when(at >= whole)
                def _():
                    block[k, :, :rest] = table[:, whole * LANES :]

        total = weights[...]
        lanes = lax.broadcasted_iota(jnp.int32, weights.shape, 1)
        for k in range(2):
            tile = 2 * pair + k
            rid = rel_ids[tile]
            w = pick_lane(block[k], rid - rid // LANES * LANES)
            w = jnp.where(tile < live, w, 0.0)
            total = jnp.where(lanes == tile, w, total)
        weights[...] = total

    rotate_pair(0, live, ent, heads, weights, out)
    put = pltpu.make_async_copy(out, query.at[pl.ds(0, 2)], sem)
    put.start()
    put.wait()


def query_kernel(count, ent, heads, weights, begun, query, out, sems):
    live = count[0, 0]
    pairs = 2 * ((live + 3) // 4)

    def put(pair):
        return pltpu.make_async_copy(out.at[pair], query.at[pl.ds(2 * pair, 2)], sems.at[pair])

    @pl.loop(1, pairs)
    def _(pair):
        rotate_pair(pair, live, ent, heads, weights, out.at[pair])
        put(pair).start()

    @pl.loop(1, pairs)
    def _(pair):
        put(pair).wait()


def tail_kernel(count, query, partner, hub, tails, pick, diff, grads, table, acc, qin, picks, diffs, moves, qsem, psem, dsem):
    dim, rows = hub.shape[0], partner.shape[1]
    edges = tails.shape[1]
    live = count[0, 0]
    quads = (live + 3) // 4
    pairs = 2 * quads

    def fetch(pair):
        both = pl.ds(2 * pair, 2)
        return pltpu.make_async_copy(query.at[both], qin.at[both], qsem.at[pair])

    def put_pick(pair, slot):
        return pltpu.make_async_copy(picks.at[slot], pick.at[pair], psem.at[slot])

    def put_diff(pair):
        both = pl.ds(2 * pair, 2)
        return pltpu.make_async_copy(diffs.at[both], diff.at[both], dsem.at[pair])

    @pl.loop(0, pairs)
    def _(pair):
        fetch(pair).start()

    table[:, :rows] = partner[:dim]
    table[:, rows:] = hub[...]
    acc[...] = jnp.zeros_like(acc)
    moves[...] = jnp.zeros_like(moves)
    eye = lax.broadcasted_iota(jnp.int32, (edges, edges), 0) == lax.broadcasted_iota(
        jnp.int32, (edges, edges), 1
    )

    def pick_tails(pair, slot):
        picks[slot] = dot_nn(table[...], hot(pair_ids(tails, pair), table.shape[1])).astype(BF)

    def spread(pair, slot):
        acc[...] += dot_nt(moves[slot], hot(pair_ids(tails, pair), table.shape[1]))

    pick_tails(0, 0)
    put_pick(0, 0).start()

    @pl.loop(0, quads)
    def _(quad):
        for slot in range(2):
            pair = 2 * quad + slot
            fetch(pair).wait()

            @pl.when(pair >= 1)
            def _():
                put_pick(pair - 1, 1 - slot).wait()

            ats = [slice(k * edges, (k + 1) * edges) for k in range(2)]
            qs = [qin[2 * pair + k] for k in range(2)]
            scores = [dot_tn(picks[slot, :, ats[k]], qs[k]) for k in range(2)]
            spread(jnp.maximum(pair - 1, 0), 1 - slot)
            ds = []
            for k in range(2):
                tile = 2 * pair + k
                top = jnp.max(scores[k], axis=0, keepdims=True)
                expo = jnp.exp(scores[k] - top)
                probs = expo * (1.0 / jnp.sum(expo, axis=0, keepdims=True))
                d = jnp.where(eye, probs - 1.0, probs)
                if slot + k:
                    d = jnp.where(tile < live, d, 0.0)
                ds.append(d.astype(BF))
                diffs[tile] = ds[k]
            pick_tails(jnp.minimum(pair + 1, pairs - 1), 1 - slot)
            for k in range(2):
                moves[slot, :, ats[k]] = dot_nt(qs[k], ds[k]).astype(BF)
            put_diff(pair).start()

            @pl.when(pair + 1 < pairs)
            def _():
                put_pick(pair + 1, 1 - slot).start()

    spread(pairs - 1, 1)
    chunks, step = grads.shape[0], grads.shape[1]
    for c in range(chunks):
        n = min(step, dim - c * step)
        grads[c, :n] = acc[c * step : c * step + n].astype(BF)
        if n < step:
            grads[c, n:] = jnp.zeros((step - n, grads.shape[2]), BF)
    put_pick(pairs - 1, 1).wait()

    @pl.loop(0, pairs)
    def _(pair):
        put_diff(pair).wait()


def head_kernel(count, pick, diff, weights, heads, acc, pin, din, moves, psem, dsem):
    half = acc.shape[0] // 2
    edges = heads.shape[1]
    live = count[0, 0]
    quads = (live + 3) // 4
    pairs = 2 * quads

    def get_pick(pair):
        return pltpu.make_async_copy(pick.at[pair], pin.at[pair], psem.at[pair])

    def get_diff(pair):
        both = pl.ds(2 * pair, 2)
        return pltpu.make_async_copy(diff.at[both], din.at[both], dsem.at[pair])

    @pl.loop(0, pairs)
    def _(pair):
        get_pick(pair).start()
        get_diff(pair).start()

    acc[...] = jnp.zeros_like(acc)
    moves[...] = jnp.zeros_like(moves)

    def spread(pair, slot):
        acc[...] += dot_nt(moves[slot], hot(pair_ids(heads, pair), acc.shape[1]))

    @pl.loop(0, quads)
    def _(quad):
        for slot in range(2):
            pair = 2 * quad + slot
            get_pick(pair).wait()
            get_diff(pair).wait()
            ats = [slice(k * edges, (k + 1) * edges) for k in range(2)]
            d_query = [dot_nn(pin[pair, :, ats[k]], din[2 * pair + k]) for k in range(2)]
            spread(jnp.maximum(pair - 1, 0), 1 - slot)
            for k in range(2):
                w = pick_lane(weights[...], 2 * pair + k)
                dr, di = d_query[k][:half], d_query[k][half:]
                wr, wi = w[:half], w[half:]
                moves[slot, :, ats[k]] = jnp.concatenate(
                    [dr * wr + di * wi, di * wr - dr * wi], axis=0
                ).astype(BF)

    spread(pairs - 1, 1)


def spread_kernel(rows, out, sem):
    put = pltpu.make_async_copy(rows, out.at[pl.ds(0, rows.shape[0])], sem)
    put.start()
    put.wait()


def reorder_kernel(matching, rows, out):
    for g in range(out.shape[0]):
        out[g] = rows[matching[g]]


def return_kernel(matching, back, hub, out):
    rows = out.shape[2] - hub.shape[2]
    total = hub[0].astype(F32)
    for m in range(1, hub.shape[0]):
        total += hub[m].astype(F32)
    total = total.astype(BF)
    for g in range(out.shape[0]):
        out[matching[g], :, :rows] = back[g, :, :rows]
        out[g, :, rows:] = total


def update_kernel(ent, hub, head_acc, last, new_ent, new_hub):
    dim, rows = ent.shape
    step = last.shape[1]
    for c in range(last.shape[0]):
        n = min(step, dim - c * step)
        at = slice(c * step, c * step + n)
        got = last[c, :n].astype(F32)
        new_ent[at] = (ent[at].astype(F32) - learn_rate * (head_acc[at] + got[:, :rows])).astype(BF)
        new_hub[at] = (hub[at].astype(F32) - learn_rate * got[:, rows:]).astype(BF)


def call(kernel, out_shape, in_specs, out_specs, flops, moved, scratch=(), exps=0, vmem=32, aliases={}):
    return pl.pallas_call(
        kernel,
        out_shape=out_shape,
        in_specs=in_specs,
        out_specs=out_specs,
        scratch_shapes=scratch,
        input_output_aliases=aliases,
        compiler_params=pltpu.CompilerParams(vmem_limit_bytes=vmem * 1024 * 1024),
        cost_estimate=pl.CostEstimate(flops=flops, bytes_accessed=moved, transcendentals=exps),
    )


shape = jax.ShapeDtypeStruct


def run_first(tile_count, tile_rel, ent, rel, head_index):
    dim, rows = ent.shape
    tiles, edges = head_index.shape
    return call(
        first_kernel,
        [shape((2 * tiles, dim, edges), BF), shape((dim, LANES), F32)],
        [SMEM, SMEM, VMEM, HBM, VMEM],
        [HBM, VMEM],
        4 * edges * dim * rows,
        4 * rel.size,
        [
            pltpu.VMEM(rel.shape, F32),
            pltpu.VMEM((2, dim, LANES), F32),
            pltpu.VMEM((2, dim, edges), BF),
            DMA(()),
            DMA(()),
        ],
        vmem=60,
    )(tile_count, tile_rel, ent, rel, head_index)


def run_query(tile_count, ent, head_index, weights, begun):
    dim, rows = ent.shape
    tiles, edges = head_index.shape
    return call(
        query_kernel,
        shape(begun.shape, BF),
        [SMEM, VMEM, VMEM, VMEM, HBM],
        HBM,
        2 * tiles * edges * dim * rows,
        2 * tiles * dim * edges,
        [pltpu.VMEM((tiles // 2, 2, dim, edges), BF), DMA((tiles // 2,))],
        vmem=60,
        aliases={4: 0},
    )(tile_count, ent, head_index, weights, begun)


def run_tail(tile_count, query, partner, hub, tail_index, groups, step):
    tiles, edges = tail_index.shape
    dim = query.shape[1]
    rows, hubs = partner.shape[1], hub.shape[1]
    return call(
        tail_kernel,
        [
            shape((tiles, dim, 2 * edges), BF),
            shape((3 * tiles, edges, edges), BF),
            shape((groups, step, rows + hubs), BF),
        ],
        [SMEM, HBM, VMEM, VMEM, VMEM],
        [HBM, HBM, VMEM],
        4 * tiles * edges * dim * (rows + hubs + edges),
        8 * tiles * dim * edges,
        [
            pltpu.VMEM((dim, rows + hubs), BF),
            pltpu.VMEM((dim, rows + hubs), F32),
            pltpu.VMEM((tiles, dim, edges), BF),
            pltpu.VMEM((2, dim, 2 * edges), BF),
            pltpu.VMEM((tiles, edges, edges), BF),
            pltpu.VMEM((2, dim, 2 * edges), BF),
            DMA((tiles // 2,)),
            DMA((2,)),
            DMA((tiles // 2,)),
        ],
        tiles * edges * edges,
        vmem=50,
    )(tile_count, query, partner, hub, tail_index)


def run_head(tile_count, pick, diff, weights, head_index, rows):
    tiles, edges = head_index.shape
    dim = pick.shape[1]
    return call(
        head_kernel,
        shape((dim, rows), F32),
        [SMEM, HBM, HBM, VMEM, VMEM],
        VMEM,
        2 * tiles * edges * dim * (rows + edges),
        6 * tiles * dim * edges,
        [
            pltpu.VMEM((tiles // 2, dim, 2 * edges), BF),
            pltpu.VMEM((tiles, edges, edges), BF),
            pltpu.VMEM((2, dim, 2 * edges), BF),
            DMA((tiles // 2,)),
            DMA((tiles // 2,)),
        ],
        vmem=60,
    )(tile_count, pick, diff, weights, head_index)


def make(groups, members):
    def shards(entities, hub_rows, relations, matching, head_index, tail_index, tile_rel, tile_count):
        ent, hub, rel = entities.T, hub_rows.T, relations.T
        dim, rows = ent.shape
        hubs = hub.shape[1]
        step = -(-dim // (8 * groups)) * 8

        cut = call(
            spread_kernel, shape((groups * step, rows), BF), [HBM], HBM, 0, 4 * ent.size, [DMA(())], vmem=62
        )(ent)
        cut = lax.all_to_all(cut.reshape(groups, step, rows), "group", 0, 0)
        query, weights = run_first(tile_count, tile_rel, ent, rel, head_index)
        cut, query, weights = lax.optimization_barrier((cut, query, weights))
        cut = call(reorder_kernel, shape(cut.shape, BF), [SMEM, VMEM], VMEM, 0, 4 * cut.size)(
            matching, cut
        )
        partner = lax.all_to_all(cut, "group", 0, 0).reshape(groups * step, rows)
        query = run_query(tile_count, ent, head_index, weights, query)
        pick, diff, grads = run_tail(tile_count, query, partner, hub, tail_index, groups, step)

        got = lax.all_to_all(grads, "group", 0, 0)
        got, pick, diff = lax.optimization_barrier((got, pick, diff))
        part = jnp.sum(got[:, :, rows:].astype(F32), axis=0).astype(BF)
        other = lax.ppermute(part, "member", [(m, m ^ 1) for m in range(members)])
        part = (part.astype(F32) + other.astype(F32)).astype(BF)
        cores = [list(range(core, members, 2)) for core in range(2)]
        parts = jnp.broadcast_to(part[None], (members // 2,) + part.shape)
        parts = lax.all_to_all(parts, "member", 0, 0, axis_index_groups=cores)
        head_acc = run_head(tile_count, pick, diff, weights, head_index, rows)
        parts, head_acc = lax.optimization_barrier((parts, head_acc))
        sent = call(
            return_kernel, shape(got.shape, BF), [SMEM, VMEM, VMEM], VMEM, 0, 4 * got.size
        )(matching, got, parts)
        last = lax.all_to_all(sent, "group", 0, 0)
        new_ent, new_hub = call(
            update_kernel,
            [shape((dim, rows), BF), shape((dim, hubs), BF)],
            [VMEM, VMEM, VMEM, VMEM],
            [VMEM, VMEM],
            0,
            8 * dim * rows,
        )(ent, hub, head_acc, last)
        return (new_ent.T, new_hub.T)

    return shards


def solution(mesh):
    placed = (
        P(("group", "member"), None),
        P(),
        P(),
        P(),
        P(("group", "member"), None),
        P(("group", "member"), None),
        P(("group", "member")),
        P("group", "member"),
    )
    return jax.shard_map(
        make(mesh.shape["group"], mesh.shape["member"]),
        mesh=mesh,
        in_specs=placed,
        out_specs=(P(("group", "member"), None), P()),
        check_vma=False,
    )
```

time: 108 us -> 106 us (0.981); the launches traced: 106 us -> 107 us
  blocking collectives: 48.5 us -> 31.5 us
  Pallas kernels: 22.3 us -> 32.6 us
  starting transfers between devices: 17.4 us -> 22.1 us
  waiting for transfers between devices: 13.7 us -> 17.2 us
    all_to_all x1 -> x0, blocking collectives: 13.1 us -> none  [shards(): partner = lax.all_to_all(cut, 'group', 0, 0).reshape(groups * step, rows)]
    pallas_call x2 -> x4, Pallas kernels: 14.3 us -> 25.1 us  [the longest x1 13.5 us: shards(): call(spread_kernel, shape((groups * step, rows), BF), [HBM], HBM, 0, 4 *...]
    all_to_all x2 -> x3, starting transfers between devices: 17.4 us -> 22 us  [the longest x1 12.9 us: shards(): parts = lax.all_to_all(parts, 'member', 0, 0, axis_index_groups=cores)]
    all_to_all x1, blocking collectives: 21.5 us -> 18.1 us  [shards(): got = lax.all_to_all(grads, 'group', 0, 0)]
    all_to_all x2 -> x3, waiting for transfers between devices: 13.7 us -> 16.1 us  [the longest x1 6.48 us: shards(): parts = lax.all_to_all(parts, 'member', 0, 0, axis_index_groups=cores)]
    pad x1 -> x0, local copies, waits for them, and re-layouts: 1.8 us -> none  [shards(): jnp.pad(ent, ((0, groups * step - dim), (0, 0))).reshape(groups, step, rows)]
    unnamed x8 -> x12, local copies, waits for them, and re-layouts: 0.02 us -> 1.82 us
    pallas_call x1, Pallas kernels: 5.82 us -> 4.56 us  [run_head(): call(head_kernel, shape((dim, rows), F32), [SMEM, HBM, HBM, VMEM, VMEM],...]
  transfers between devices with their start and end apart: 2 -> 4, of which waited for: 2 -> 4; matrix products, arithmetic and copies ran while one was open for 0% -> 0% of each run, Pallas kernels for 10% -> 11%
where the time goes in v3:
time: 106 us; the launch traced here: 107 us
  Pallas kernels  32.6 us (31%)
  blocking collectives  31.5 us (30%)
  starting transfers between devices  22.1 us (21%)
  waiting for transfers between devices  17.2 us (16%)
  local copies, waits for them, and re-layouts  2.54 us (2%)
  between operations  1.38 us (1%)
    all_to_all x1, blocking collectives, shards(): got = lax.all_to_all(grads, 'group', 0, 0)  18.1 us
    pallas_call x1, Pallas kernels, shards(): call(spread_kernel, shape((groups * step, rows), BF), [HBM], HBM, 0, 4 *...  13.5 us
    all_to_all x1, blocking collectives, shards(): last = lax.all_to_all(sent, 'group', 0, 0)  13.4 us
    all_to_all x1, starting transfers between devices, shards(): parts = lax.all_to_all(parts, 'member', 0, 0, axis_index_groups=cores)  12.9 us
    all_to_all x1, waiting for transfers between devices, shards(): parts = lax.all_to_all(parts, 'member', 0, 0, axis_index_groups=cores)  6.48 us
    all_to_all x1, waiting for transfers between devices, shards(): partner = lax.all_to_all(cut, 'group', 0, 0).reshape(groups * step, rows)  6.32 us
    all_to_all x1, starting transfers between devices, shards(): cut = lax.all_to_all(cut.reshape(groups, step, rows), 'group', 0, 0)  5.67 us
    pallas_call x1, Pallas kernels, run_first(): call(first_kernel, [shape((2 * tiles, dim, edges), BF), shape((dim, LANES...  5.14 us
  transfers between devices with their start and end apart: 4, of which 4 were waited for; matrix products, arithmetic and copies ran while one was open for 0% of the time, Pallas kernels for 11%

profile of v3, /device:TPU:64, one launch (start us, length us, event | category | flops | bytes accessed | tf_op | source)
XLA Modules:
  0.0 107.3 jit_solution(12266966201327483439)
XLA Ops:
  0.6 13.5 %shard_map.95 = bf16[448,512]{1,0:T(8,128)(2,1)} custom-call(bf16[400,512]{1,0:T(8,128)(2,1)} %bitcast.7), custom_call_target="tpu_custom_call" | custom-call | bytes 819200 | tf_op jit(solution)/shard_map/pallas_call | solution.py:390
  14.2 5.7 %all-to-all-start = ((bf16[8,56,512]{2,1,0:T(8,128)(2,1)}), bf16[8,56,512]{2,1,0:T(8,128)(2,1)S(1)}, u32[]{:S(2)}, u32[]{:S(2)}) async-start(bf16[8,56,512]{2,1,0:T(8,128)(2,1)} %bitcast.15), calls=%async_computation | async-start | bytes 917504 | tf_op jit(solution)/shard_map/all_to_all | solution.py:393
  20.5 5.1 %shard_map.96 = (bf16[32,400,256]{2,1,0:T(8,128)(2,1)}, f32[400,128]{1,0:T(8,128)}) custom-call(s32[1,1]{1,0:T(1,128)S(6)} %copy.12.count, s32[16]{0:T(128)} %rel_ids.1, bf16[400,512]{1,0:T(8,128)(2,1)} %bitcast.8, f32[400,2112]{1,0:T(8,128)} %bitcast.14, s32[16,256]{1,0:T(8,128)} %heads.5), custom_call_target="tpu_custom_call" | custom-call | flops 209715200 | bytes 3379200 | tf_op jit(solution)/shard_map/pallas_call | solution.py:297
  25.6 3.3 %all-to-all-done.rows = bf16[8,56,512]{2,1,0:T(8,128)(2,1)S(1)} async-done(((bf16[8,56,512]{2,1,0:T(8,128)(2,1)}), bf16[8,56,512]{2,1,0:T(8,128)(2,1)S(1)}, u32[]{:S(2)}, u32[]{:S(2)}) %all-to-all-start) | async-done | bytes 458784 | tf_op jit(solution)/shard_map/all_to_all | solution.py:393
  28.9 0.7 copy-done.3
  29.5 1.4 %shard_map.98 = bf16[8,56,512]{2,1,0:T(8,128)(2,1)} custom-call(s32[8]{0:T(128)S(1)} %copy-done.3, bf16[8,56,512]{2,1,0:T(8,128)(2,1)S(1)} %all-to-all-done.rows), custom_call_target="tpu_custom_call" | custom-call | bytes 917504 | tf_op jit(solution)/shard_map/pallas_call | solution.py:396
  30.9 3.5 %all-to-all-start.1 = ((bf16[8,56,512]{2,1,0:T(8,128)(2,1)}), bf16[8,56,512]{2,1,0:T(8,128)(2,1)S(1)}, u32[]{:S(2)}, u32[]{:S(2)}) async-start(bf16[8,56,512]{2,1,0:T(8,128)(2,1)} %shard_map.98), calls=%async_computation.1 | async-start | bytes 917504 | tf_op jit(solution)/shard_map/all_to_all | solution.py:399
  34.4 0.0 copy-start.2
  34.4 0.0 copy-start.5
  34.4 2.4 %shard_map.97.query = bf16[32,400,256]{2,1,0:T(8,128)(2,1)} custom-call(s32[1,1]{1,0:T(1,128)S(6)} %copy.12.count, bf16[400,512]{1,0:T(8,128)(2,1)} %bitcast.9, s32[16,256]{1,0:T(8,128)} %heads.5, f32[400,128]{1,0:T(8,128)} %get-tuple-element.19.weights, bf16[32,400,256]{2,1,0:T(8,128)(2,1)} %get-tuple-element.20.begun), custom_call_target="tpu_custom_call", output_to_operand_aliasing={{}: (4, {})} | custom-call | flops 1677721600 | bytes 3276800 | tf_op jit(solution)/shard_map/pallas_call | solution.py:318
  36.8 6.3 %all-to-all-done.1 = bf16[8,56,512]{2,1,0:T(8,128)(2,1)S(1)} async-done(((bf16[8,56,512]{2,1,0:T(8,128)(2,1)}), bf16[8,56,512]{2,1,0:T(8,128)(2,1)S(1)}, u32[]{:S(2)}, u32[]{:S(2)}) %all-to-all-start.1) | async-done | bytes 458784 | tf_op jit(solution)/shard_map/all_to_all | solution.py:399
  43.1 4.0 %shard_map.99 = (bf16[16,400,512]{2,1,0:T(8,128)(2,1)}, bf16[48,256,256]{2,1,0:T(8,128)(2,1)}, bf16[8,56,640]{2,1,0:T(8,128)(2,1)S(1)}) custom-call(s32[1,1]{1,0:T(1,128)S(6)} %copy.12.count, bf16[32,400,256]{2,1,0:T(8,128)(2,1)} %shard_map.97.query, bf16[448,512]{1,0:T(8,128)(2,1)S(1)} %bitcast.11, bf16[400,128]{1,0:T(8,128)(2,1)S(1)} %bitcast.12, ...), custom_call_target="tpu_custom_call" | custom-call | flops 5872025600 | bytes 13107200 | tf_op jit(solution)/shard_map/pallas_call | solution.py:335
  47.1 18.1 %all_to_all.25.back = bf16[8,56,640]{2,1,0:T(8,128)(2,1)S(1)} all-to-all(bf16[8,56,640]{2,1,0:T(8,128)(2,1)S(1)} %get-tuple-element.22), channel_id=1, replica_groups=mesh['group'=8,'member'=32] {'group'}, dimensions={0} | all-to-all | bytes 1146880 | tf_op jit(solution)/shard_map/all_to_all | solution.py:403
  65.2 0.1 collective-permute-start
  65.3 1.2 %collective-permute-done = bf16[56,128]{1,0:T(8,128)(2,1)S(1)} collective-permute-done((bf16[56,128]{1,0:T(8,128)(2,1)S(1)}, bf16[56,128]{1,0:T(8,128)(2,1)S(1)}, u32[]{:S(2)}, u32[]{:S(2)}) %collective-permute-start) | collective-permute-done | bytes 14368 | tf_op jit(solution)/shard_map/ppermute | solution.py:406
  66.5 0.7 broadcast_in_dim.2
  67.2 12.9 %all-to-all-start.3 = ((bf16[16,56,128]{2,1,0:T(8,128)(2,1)}), bf16[16,56,128]{2,1,0:T(8,128)(2,1)S(1)}, u32[]{:S(2)}, u32[]{:S(2)}) async-start(bf16[16,56,128]{2,1,0:T(8,128)(2,1)} %broadcast_in_dim.2), calls=%async_computation.3 | async-start | bytes 458752 | tf_op jit(solution)/shard_map/all_to_all | solution.py:410
  80.1 0.0 copy-start
  80.1 4.6 %shard_map.100.head_acc = f32[400,512]{1,0:T(8,128)} custom-call(s32[1,1]{1,0:T(1,128)S(6)} %copy.12.count, bf16[16,400,512]{2,1,0:T(8,128)(2,1)} %get-tuple-element.26.pick, bf16[48,256,256]{2,1,0:T(8,128)(2,1)} %get-tuple-element.27.diff, f32[400,128]{1,0:T(8,128)} %get-tuple-element.19.weights, s32[16,256]{1,0:T(8,128)} %heads.5), custom_call_target="tpu_custom_call" | custom-call | flops 2516582400 | bytes 9830400 | tf_op jit(solution)/shard_map/pallas_call | solution.py:365
  84.7 6.5 %all-to-all-done.3.hub = bf16[16,56,128]{2,1,0:T(8,128)(2,1)S(1)} async-done(((bf16[16,56,128]{2,1,0:T(8,128)(2,1)}), bf16[16,56,128]{2,1,0:T(8,128)(2,1)S(1)}, u32[]{:S(2)}, u32[]{:S(2)}) %all-to-all-start.3) | async-done | bytes 229408 | tf_op jit(solution)/shard_map/all_to_all | solution.py:410
  91.2 0.6 shard_map.101
  91.8 13.4 %all_to_all.26.last = bf16[8,56,640]{2,1,0:T(8,128)(2,1)S(1)} all-to-all(bf16[8,56,640]{2,1,0:T(8,128)(2,1)S(1)} %shard_map.101), channel_id=1, replica_groups=mesh['group'=8,'member'=32] {'group'}, dimensions={0} | all-to-all | bytes 1146880 | tf_op jit(solution)/shard_map/all_to_all | solution.py:416
  105.2 1.1 %copy-done.1 = f32[400,512]{1,0:T(8,128)S(1)} copy-done((f32[400,512]{1,0:T(8,128)S(1)}, f32[400,512]{1,0:T(8,128)}, u32[]{:S(2)}) %copy-start.1) | copy-done | bytes 819224
  106.4 1.0 shard_map.102
  (9 shorter events, 0.0 us)
Async XLA Ops:
  14.2 14.7 %all-to-all-start = ((bf16[8,56,512]{2,1,0:T(8,128)(2,1)}), bf16[8,56,512]{2,1,0:T(8,128)(2,1)S(1)}, u32[]{:S(2)}, u32[]{:S(2)}) async-start(bf16[8,56,512]{2,1,0:T(8,128)(2,1)} %bitcast.15), calls=%async_computation | async-start | bytes 917504 | tf_op jit(solution)/shard_map/all_to_all | solution.py:393
  28.9 0.7 copy-start.3
  30.9 12.2 %all-to-all-start.1 = ((bf16[8,56,512]{2,1,0:T(8,128)(2,1)}), bf16[8,56,512]{2,1,0:T(8,128)(2,1)S(1)}, u32[]{:S(2)}, u32[]{:S(2)}) async-start(bf16[8,56,512]{2,1,0:T(8,128)(2,1)} %shard_map.98), calls=%async_computation.1 | async-start | bytes 917504 | tf_op jit(solution)/shard_map/all_to_all | solution.py:399
  34.4 8.7 %copy-start.2 = (bf16[128,400]{0,1:T(8,128)(2,1)S(1)}, bf16[128,400]{0,1:T(8,128)(2,1)}, u32[]{:S(2)}) copy-start(bf16[128,400]{0,1:T(8,128)(2,1)} %param.9) | copy-start | bytes 307204
  34.4 8.7 %copy-start.5 = (s32[16,256]{1,0:T(8,128)S(1)}, s32[16,256]{1,0:T(8,128)}, u32[]{:S(2)}) copy-start(s32[16,256]{1,0:T(8,128)} %tails.1) | copy-start | bytes 49156
  65.2 1.3 %collective-permute-start = (bf16[56,128]{1,0:T(8,128)(2,1)S(1)}, bf16[56,128]{1,0:T(8,128)(2,1)S(1)}, u32[]{:S(2)}, u32[]{:S(2)}) collective-permute-start(bf16[56,128]{1,0:T(8,128)(2,1)S(1)} %slice_reduce_fusion), channel_id=1, source_target_pairs={{0,1},{1,0},{2,3},{3,2},{4,5},{5,4},{6,7},{7,6},{8,9},{9,8},{10,11... | collective-permute-start | bytes 43016 | tf_op jit(solution)/shard_map/ppermute | solution.py:406
  67.2 24.0 %all-to-all-start.3 = ((bf16[16,56,128]{2,1,0:T(8,128)(2,1)}), bf16[16,56,128]{2,1,0:T(8,128)(2,1)S(1)}, u32[]{:S(2)}, u32[]{:S(2)}) async-start(bf16[16,56,128]{2,1,0:T(8,128)(2,1)} %broadcast_in_dim.2), calls=%async_computation.3 | async-start | bytes 458752 | tf_op jit(solution)/shard_map/all_to_all | solution.py:410
  80.1 11.1 %copy-start.4 = (s32[8]{0:T(128)S(1)}, s32[8]{0:T(128)}, u32[]{:S(2)}) copy-start(s32[8]{0:T(128)} %matching.3) | copy-start | bytes 100
  80.1 25.1 %copy-start = (bf16[512,400]{0,1:T(8,128)(2,1)S(1)}, bf16[512,400]{0,1:T(8,128)(2,1)}, u32[]{:S(2)}) copy-start(bf16[512,400]{0,1:T(8,128)(2,1)} %param.8) | copy-start | bytes 1228804
  105.2 1.1 %copy-start.1 = (f32[400,512]{1,0:T(8,128)S(1)}, f32[400,512]{1,0:T(8,128)}, u32[]{:S(2)}) copy-start(f32[400,512]{1,0:T(8,128)} %shard_map.100.head_acc) | copy-start | bytes 2457604
